TPU v7x, 32 devices: a whole 2x2x4 slice. The times are simulated.
32 devices in a mesh: beam: 8 (over z, y), elem: 4 (over x, core).
Axes of the slice: x: 2, y: 2, z: 4, core: 2. Of those that a mesh axis runs over, the one named last changes fastest.
Arguments:
- signals: bfloat16 [2, 16384, 256], P(None, 'elem', 'beam'), may hold values from -6 to 6
- weights: bfloat16 [2, 16384, 16384], P(None, 'beam', 'elem'), may hold values from -0.0625 to 0.0625
- element_flags: int32 [16384], P('elem'), may hold values from 0 to 1, as said below
Outputs:
- beam_out: bfloat16 [2, 16384, 256], P(None, ('beam', 'elem'))
- beam_power: float32 [16384], P(('beam', 'elem'))
Inputs may be any that keep to these rules, and one draw needn't show every extreme that they name: `element_flags`: element 16384 - 1 is always live.
All inputs are finite; a program needn't handle non-finite values.
Results may differ from a plain program's by a relative error of at most 0.001.
Values may be sent and summed in bfloat16 or wider, within the bound.
A program may use at most 128 MiB of HBM per device.

v0:
```python
import functools

import jax
import jax.numpy as jnp
from jax import lax
from jax.experimental import pallas as pl
from jax.experimental.pallas import tpu as pltpu
from jax.sharding import PartitionSpec as P

PIECES = 4
LANES = 128
SPLIT = 2
MESH = pl.DeviceIdType.MESH


def ring_order(mesh):
    nb = mesh.shape["beam"]
    try:
        coords = [tuple(d.coords) for d in mesh.devices[:, 0]]
    except AttributeError:
        return list(range(nb))
    axes = [a for a in range(len(coords[0])) if len({c[a] for c in coords}) > 1]
    if len(axes) != 2:
        return list(range(nb))
    values = [sorted({c[a] for c in coords}) for a in axes]
    if len(values[0]) % 2:
        axes, values = axes[::-1], values[::-1]
    rows, cols = len(values[0]), len(values[1])
    if rows % 2 or rows * cols != nb:
        return list(range(nb))
    at = {(values[0].index(c[axes[0]]), values[1].index(c[axes[1]])): i for i, c in enumerate(coords)}
    path = [(0, 0)]
    for r in range(rows):
        inner = range(1, cols) if r % 2 == 0 else range(cols - 1, 0, -1)
        path += [(r, c) for c in inner]
    path += [(r, 0) for r in range(rows - 1, 0, -1)]
    return [at[p] for p in path]


def lookup(table, index):
    value = jnp.int32(table[0])
    for i in range(1, len(table)):
        value = jnp.where(index == i, jnp.int32(table[i]), value)
    return value


def kernel(order, ne, s_ref, flag_ref, w_ref, out_ref, pow_ref,
           blocks, mask, weights, rhs, part, first, second, counts,
           ring_send, ring_recv, w_sem, s_sem, first_send, first_recv, second_send, second_recv,
           cnt_send, cnt_recv):
    nb = len(order)
    half = nb // 2
    _, tb, depth = s_ref.shape
    q = PIECES
    two_t, kq = 2 * tb, depth // q
    chunks, _, mo, width = part.shape
    group = width // two_t
    ways = ne // 2
    snaps = nb * tb

    me_b = lax.axis_index("beam")
    me_e = lax.axis_index("elem")
    inverse = [order.index(i) for i in range(nb)]
    pos = lookup(inverse, me_b)
    ahead = lookup([order[(inverse[i] + 1) % nb] for i in range(nb)], me_b)
    behind = lookup([order[(inverse[i] - 1) % nb] for i in range(nb)], me_b)
    core = lax.rem(me_e, 2)
    mine = me_e // 2
    partner = me_e + 1 - 2 * core

    def slot_of(way, d):
        return d if (way == 0 or d in (0, half)) else half + d

    if half == 4:
        arrivals = [[(1, 0), (1, 1), (2, 0), (1, 2), (2, 1), (1, 3), (2, 2), (2, 3),
                     (3, 0), (3, 1), (3, 2), (3, 3), (4, 2), (4, 3)],
                    [(1, 0), (1, 1), (2, 0), (1, 2), (3, 0), (1, 3), (2, 1), (4, 0),
                     (3, 1), (2, 2), (4, 1), (2, 3), (3, 2), (3, 3)]]
    else:
        last = (((half - 1, 0), (half - 1, 1), (half - 1, 2), (half - 1, 3), (half, 2), (half, 3)),
                ((half - 1, 0), (half - 1, 1), (half, 0), (half - 1, 2), (half, 1), (half - 1, 3)))
        arrivals = [[(d, j) for d in range(1, half - 1) for j in range(q)]
                    + [(d, j) for d, j in last[way] if d > 0] for way in (0, 1)]
    number = [{item: k for k, item in enumerate(a)} for a in arrivals]

    def ring_copy(way, d, j):
        k = number[way][(d, j)]
        return pltpu.make_async_remote_copy(
            src_ref=(s_ref if d == 1 else blocks.at[slot_of(way, d - 1)]).at[:, :, pl.ds(j * kq, kq)],
            dst_ref=blocks.at[slot_of(way, d), :, :, pl.ds(j * kq, kq)],
            send_sem=ring_send.at[way, k], recv_sem=ring_recv.at[way, k],
            device_id={"beam": ahead if way == 0 else behind}, device_id_type=MESH)

    def weight_copy(i, j):
        return pltpu.make_async_copy(
            w_ref.at[i, :, pl.ds(j * kq, kq)], weights.at[j, :, pl.ds(i * kq, kq)], w_sem.at[i, j])

    def count_copy(r):
        return pltpu.make_async_remote_copy(
            src_ref=flag_ref, dst_ref=counts.at[r - 1], send_sem=cnt_send.at[r - 1], recv_sem=cnt_recv.at[r - 1],
            device_id={"elem": lax.rem(me_e + r, ne)}, device_id_type=MESH)

    def kept(i):
        return 2 * lax.rem(mine + i, ways) + core

    def given(i):
        return 2 * lax.rem(mine + i, ways) + 1 - core

    def first_copy(c, i):
        return pltpu.make_async_remote_copy(
            src_ref=part.at[c, given(i)], dst_ref=first.at[c, i],
            send_sem=first_send.at[c, i], recv_sem=first_recv.at[c, i],
            device_id={"elem": partner}, device_id_type=MESH)

    def parts_of(c):
        return SPLIT if c == chunks - 1 else 1

    def rows_of(c, h):
        size = mo // parts_of(c)
        return slice(h * size, (h + 1) * size)

    def second_copy(c, i, h):
        rows = pl.ds(h * (mo // parts_of(c)), mo // parts_of(c))
        return pltpu.make_async_remote_copy(
            src_ref=first.at[c, i, rows], dst_ref=second.at[c, i - 1, rows],
            send_sem=second_send.at[c, i - 1, h], recv_sem=second_recv.at[c, i - 1, h],
            device_id={"elem": kept(i)}, device_id_type=MESH)

    own_in = pltpu.make_async_copy(s_ref, blocks.at[0], s_sem)
    own_in.start()

    barrier = pltpu.get_barrier_semaphore()
    for b in (ahead, behind):
        pl.semaphore_signal(barrier, inc=1, device_id={"beam": b}, device_id_type=MESH)
    for r in range(1, ne):
        pl.semaphore_signal(barrier, inc=1, device_id={"elem": lax.rem(me_e + r, ne)}, device_id_type=MESH)
    pl.semaphore_wait(barrier, 2 + ne - 1)

    arrived = {((0, 0), j) for j in range(q)}
    sent = [0, 0]

    def send_ready():
        for way in (0, 1):
            while sent[way] < len(arrivals[way]):
                d, j = arrivals[way][sent[way]]
                if d > 1 and ((way, d - 1), j) not in arrived:
                    break
                ring_copy(way, d, j).start()
                sent[way] += 1

    send_ready()
    for r in range(1, ne):
        count_copy(r).start()
    for j in range(q):
        for i in (0, 1):
            weight_copy(i, j).start()

    mask[...] = jnp.broadcast_to(flag_ref[...].astype(jnp.float32).astype(jnp.bfloat16), mask.shape)
    own_in.wait()

    sequence = [(0, 0)]
    for d in range(1, half):
        sequence += [(0, d), (1, d)]
    sequence += [(0, half)]

    def members(c):
        return sequence[c * group:(c + 1) * group]

    def stage(c, j):
        for s, (way, d) in enumerate(members(c)):
            columns = pl.ds(j * kq, kq)
            re = blocks[slot_of(way, d), 0, :, columns] * mask[:, columns]
            im = blocks[slot_of(way, d), 1, :, columns] * mask[:, columns]
            lo, hi = s * tb, (group + s) * tb
            rhs[lo:lo + tb, :kq] = re
            rhs[hi:hi + tb, :kq] = im
            rhs[lo:lo + tb, kq:] = -im
            rhs[hi:hi + tb, kq:] = re

    def multiply(c, j, o, fresh):
        rows = pl.ds(pl.multiple_of(o * mo, mo), mo)
        product = lax.dot_general(weights[j, rows, :], rhs[...], (((1,), (1,)), ((), ())),
                                  preferred_element_type=jnp.float32)
        if fresh:
            part[c, o] = product
        else:
            part[c, o] += product

    pieces_done = [0] * chunks
    weights_here = set()
    waiting = []

    def pass_on(c, i):
        first_copy(c, i).wait_recv()
        for h in range(parts_of(c)):
            rows = rows_of(c, h)
            first[c, i, rows] += part[c, kept(i), rows]
            second_copy(c, i, h).start()

    def piece(c, j):
        stage(c, j)
        if j not in weights_here:
            weights_here.add(j)
            for i in (0, 1):
                weight_copy(i, j).wait()
        fresh = pieces_done[c] == 0
        pieces_done[c] += 1
        if pieces_done[c] < q:
            @pl.loop(0, ne)
            def _(o):
                multiply(c, j, o, fresh)
            return
        for i in list(range(1, ways)) + [0]:
            multiply(c, j, given(i), fresh)
            first_copy(c, i).start()
        for i in range(1, ways):
            multiply(c, j, kept(i), fresh)
            if c == chunks - 1:
                pass_on(c, i)
        multiply(c, j, kept(0), fresh)
        if c < chunks - 1:
            waiting.append(c)

    todo = [(c, j) for c in range(chunks) for j in range(q)]

    def run_ready():
        for c, j in list(todo):
            if all((m, j) in arrived for m in members(c)):
                todo.remove((c, j))
                piece(c, j)

    for k in range(len(arrivals[0])):
        for way in (0, 1):
            d, j = arrivals[way][k]
            ring_copy(way, d, j).wait_recv()
            arrived.add(((0 if d == half else way, d), j))
            send_ready()
        for c in waiting:
            for i in range(1, ways):
                pass_on(c, i)
        waiting.clear()
        run_ready()
    for c in waiting:
        for i in range(1, ways):
            pass_on(c, i)
    waiting.clear()

    live = flag_ref[...].astype(jnp.float32)
    for r in range(1, ne):
        count_copy(r).wait()
        live = live + counts[r - 1].astype(jnp.float32)
    gain = jnp.sqrt(jnp.float32(depth * ne) / jnp.sum(live, axis=1, keepdims=True))

    def selection(c):
        column = lax.broadcasted_iota(jnp.int32, (width, 2 * snaps), 0)
        target = lax.broadcasted_iota(jnp.int32, (width, 2 * snaps), 1)
        wanted = column
        for s, (way, d) in enumerate(members(c)):
            source = lookup(order, lax.rem(pos + (d if way else nb - d), nb))
            for p in (0, 1):
                lo = (p * group + s) * tb
                inside = (column >= lo) & (column < lo + tb)
                wanted = jnp.where(inside, column - lo + p * snaps + source * tb, wanted)
        return jnp.where(wanted == target, 1.0, 0.0).astype(jnp.bfloat16)

    def finished(c, h):
        rows = rows_of(c, h)
        value = part[c, me_e, rows] + first[c, 0, rows]
        for i in range(1, ways):
            second_copy(c, i, h).wait_recv()
            value = value + second[c, i - 1, rows]
        return value * gain

    square = jnp.zeros((mo, width), jnp.float32)
    moved = jnp.zeros((mo, 2 * snaps), jnp.float32)
    for c in range(chunks - 1):
        first_copy(c, 0).wait_recv()
        value = finished(c, 0)
        square = square + value * value
        moved = moved + jnp.dot(value.astype(jnp.bfloat16), selection(c), preferred_element_type=jnp.float32)
    c = chunks - 1
    select = selection(c)
    first_copy(c, 0).wait_recv()
    squares = []
    for h in range(SPLIT):
        rows = rows_of(c, h)
        value = finished(c, h)
        squares.append(square[rows] + value * value)
        all_moved = moved[rows] + jnp.dot(value.astype(jnp.bfloat16), select, preferred_element_type=jnp.float32)
        out_ref[0, rows] = all_moved[:, :snaps].astype(jnp.bfloat16)
        out_ref[1, rows] = all_moved[:, snaps:].astype(jnp.bfloat16)
    power = jnp.concatenate([jnp.sum(v, axis=1, keepdims=True) for v in squares], axis=0) * (1.0 / snaps)
    pow_ref[...] = jnp.broadcast_to(power, (mo, LANES)).T[0:1, :]

    for way in (0, 1):
        for d, j in arrivals[way]:
            ring_copy(way, d, j).wait_send()
    for c in range(chunks):
        for i in range(ways):
            first_copy(c, i).wait_send()
        for i in range(1, ways):
            for h in range(parts_of(c)):
                second_copy(c, i, h).wait_send()


def body(order, ne, signals, weights, element_flags):
    nb = len(order)
    _, depth, tb = signals.shape
    rows = weights.shape[1]
    mo = rows // ne
    q = PIECES
    kq = depth // q
    group = min(nb, max(1, LANES // tb))
    chunks = nb // group
    width = 2 * group * tb
    ways = ne // 2
    items = q * (nb // 2) - q // 2
    dma = pltpu.SemaphoreType.DMA
    anywhere = pl.BlockSpec(memory_space=pltpu.MemorySpace.HBM)
    vmem = pl.BlockSpec(memory_space=pltpu.VMEM)
    out, power = pl.pallas_call(
        functools.partial(kernel, order, ne),
        out_shape=(jax.ShapeDtypeStruct((2, mo, nb * tb), jnp.bfloat16),
                   jax.ShapeDtypeStruct((1, mo), jnp.float32)),
        in_specs=[anywhere, vmem, anywhere],
        out_specs=(vmem, vmem),
        scratch_shapes=[
            pltpu.VMEM((nb, 2, tb, depth), jnp.bfloat16),
            pltpu.VMEM((tb, depth), jnp.bfloat16),
            pltpu.VMEM((q, rows, 2 * kq), jnp.bfloat16),
            pltpu.VMEM((width, 2 * kq), jnp.bfloat16),
            pltpu.VMEM((chunks, ne, mo, width), jnp.float32),
            pltpu.VMEM((chunks, ways, mo, width), jnp.float32),
            pltpu.VMEM((chunks, max(1, ways - 1), mo, width), jnp.float32),
            pltpu.VMEM((ne - 1, 1, depth), jnp.int32),
            dma((2, items)), dma((2, items)), dma((2, q)), dma,
            dma((chunks, ways)), dma((chunks, ways)),
            dma((chunks, max(1, ways - 1), SPLIT)), dma((chunks, max(1, ways - 1), SPLIT)),
            dma((ne - 1,)), dma((ne - 1,)),
        ],
        compiler_params=pltpu.CompilerParams(
            collective_id=0, has_side_effects=True, vmem_limit_bytes=50 * 2**20),
        name="beamform",
    )(signals.transpose(0, 2, 1), element_flags.reshape(1, depth), weights)
    return out, power.reshape(mo)


def solution(mesh):
    return jax.shard_map(
        functools.partial(body, ring_order(mesh), mesh.shape["elem"]),
        mesh=mesh,
        in_specs=(P(None, "elem", "beam"), P(None, "beam", "elem"), P("elem")),
        out_specs=(P(None, ("beam", "elem"), None), P(("beam", "elem"))),
        check_vma=False,
    )
```

profile of v0, /device:TPU:0, one launch (start us, length us, event | category | flops | bytes accessed | tf_op | source)
XLA Modules:
  0.0 67.6 jit_solution(10056880764691397294)
XLA Ops:
  0.6 0.0 copy-start
  0.6 1.0 %copy-done = bf16[2,4096,32]{1,2,0:T(8,128)(2,1)S(1)} copy-done((bf16[2,4096,32]{1,2,0:T(8,128)(2,1)S(1)}, bf16[2,4096,32]{1,2,0:T(8,128)(2,1)}, u32[]{:S(2)}) %copy-start) | copy-done | bytes 524312
  1.7 0.0 copy-start.1
  1.7 0.7 %copy-done.1 = s32[4096]{0:T(1024)S(1)} copy-done((s32[4096]{0:T(1024)S(1)}, s32[4096]{0:T(1024)}, u32[]{:S(2)}) %copy-start.1) | copy-done | bytes 16408
  2.4 63.9 %beamform.1 = (bf16[2,512,256]{2,1,0:T(8,128)(2,1)S(1)}, f32[1,512]{1,0:T(1,128)S(1)}) custom-call(bf16[2,32,4096]{2,1,0:T(8,128)(2,1)S(1)} %bitcast.3, s32[1,4096]{1,0:T(1,128)S(1)} %bitcast.4, bf16[2,2048,4096]{2,1,0:T(8,128)(2,1)} %w_ref.1), custom_call_target="tpu_custom_call" | custom-call | tf_op jit(solution)/shard_map/beamform/pallas_call | solution.py:321
  66.3 0.8 %copy.7 = bf16[2,512,256]{2,1,0:T(8,128)(2,1)} copy(bf16[2,512,256]{2,1,0:T(8,128)(2,1)S(1)} %get-tuple-element.8) | data formatting | bytes 1048576
  67.1 0.6 copy.8
Async XLA Ops:
  0.6 1.0 %copy-start = (bf16[2,4096,32]{1,2,0:T(8,128)(2,1)S(1)}, bf16[2,4096,32]{1,2,0:T(8,128)(2,1)}, u32[]{:S(2)}) copy-start(bf16[2,4096,32]{1,2,0:T(8,128)(2,1)} %param.3) | copy-start | bytes 1572868
  1.7 0.7 %copy-start.1 = (s32[4096]{0:T(1024)S(1)}, s32[4096]{0:T(1024)}, u32[]{:S(2)}) copy-start(s32[4096]{0:T(1024)} %param.5) | copy-start | bytes 49156
where the time goes:
time: 67.9 us; the launch traced here: 67.6 us
  Pallas kernels  63.9 us (94%)
  local copies, waits for them, and re-layouts  3.13 us (5%)
    pallas_call x1, Pallas kernels, body(): pl.pallas_call(functools.partial(kernel, order, ne), out_shape=(jax.Shape...  63.9 us
    unnamed x6, local copies, waits for them, and re-layouts  3.13 us

commit v1 on v0

v1 whole, which is shorter than its diff:
```python
import functools

import jax
import jax.numpy as jnp
from jax import lax
from jax.experimental import pallas as pl
from jax.experimental.pallas import tpu as pltpu
from jax.sharding import PartitionSpec as P

PIECES = 8
LANES = 128
MESH = pl.DeviceIdType.MESH


def ring_order(mesh):
    nb = mesh.shape["beam"]
    try:
        coords = [tuple(d.coords) for d in mesh.devices[:, 0]]
    except AttributeError:
        return list(range(nb))
    axes = [a for a in range(len(coords[0])) if len({c[a] for c in coords}) > 1]
    if len(axes) != 2:
        return list(range(nb))
    values = [sorted({c[a] for c in coords}) for a in axes]
    if len(values[0]) % 2:
        axes, values = axes[::-1], values[::-1]
    rows, cols = len(values[0]), len(values[1])
    if rows % 2 or rows * cols != nb:
        return list(range(nb))
    at = {(values[0].index(c[axes[0]]), values[1].index(c[axes[1]])): i for i, c in enumerate(coords)}
    path = [(0, 0)]
    for r in range(rows):
        inner = range(1, cols) if r % 2 == 0 else range(cols - 1, 0, -1)
        path += [(r, c) for c in inner]
    path += [(r, 0) for r in range(rows - 1, 0, -1)]
    return [at[p] for p in path]


def lookup(table, index):
    value = jnp.int32(table[0])
    for i in range(1, len(table)):
        value = jnp.where(index == i, jnp.int32(table[i]), value)
    return value


def kernel(order, ne, s_ref, flag_ref, w_ref, out_ref, pow_ref,
           blocks, flags, mask, weights, rhs, xpart, opart, first, ofirst, second, counts, select, values, square,
           ring_send, ring_recv, w_sem, s_sem, f_sem, first_send, first_recv, ofirst_send, ofirst_recv,
           second_send, second_recv, cnt_send, cnt_recv):
    nb = len(order)
    half = nb // 2
    _, tb, depth = s_ref.shape
    q = PIECES
    step = max(1, q // 4)
    kq = depth // q
    mo = opart.shape[2]
    ways = ne // 2
    snaps = nb * tb
    blk = 2 * tb

    me_b = lax.axis_index("beam")
    me_e = lax.axis_index("elem")
    inverse = [order.index(i) for i in range(nb)]
    pos = lookup(inverse, me_b)
    ahead = lookup([order[(inverse[i] + 1) % nb] for i in range(nb)], me_b)
    behind = lookup([order[(inverse[i] - 1) % nb] for i in range(nb)], me_b)
    core = lax.rem(me_e, 2)
    mine = me_e // 2
    partner = me_e + 1 - 2 * core

    def slot_of(way, d):
        return d if (way == 0 or d in (0, half)) else half + d

    def unit_columns(u):
        if u == 0:
            return [(0, 0), (0, 1)]
        if u == 1:
            return [(1, 1), (1, 1)]
        if u == half:
            return [(0, half), (0, half)]
        return [(1, u), (0, u)]

    def folded(u):
        return u in (1, half)

    def place(u):
        return 1 if u == half else u

    def rows_of(u):
        return pl.ds(mo // 2 if u == half else 0, mo // 2 if folded(u) else mo)

    def pair_columns(p):
        return [(0, 0), (0, 1)] if p == 0 else [(1, p), (0, p + 1)]

    def units_of(d):
        return [0, 1] if d == 1 else [d]

    low, high = q // 2, q // 2
    arrivals = [[(d, j) for d in range(1, half) for j in range(q)] + [(half, j) for j in last]
                for last in (range(q - 1, high - 1, -1), range(low))]
    number = [{item: k for k, item in enumerate(a)} for a in arrivals]

    def ring_copy(way, d, j):
        k = number[way][(d, j)]
        return pltpu.make_async_remote_copy(
            src_ref=(s_ref if d == 1 else blocks.at[slot_of(way, d - 1)]).at[:, :, pl.ds(j * kq, kq)],
            dst_ref=blocks.at[slot_of(way, d), :, :, pl.ds(j * kq, kq)],
            send_sem=ring_send.at[way, k], recv_sem=ring_recv.at[way, k],
            device_id={"beam": ahead if way == 0 else behind}, device_id_type=MESH)

    def weight_copy(i, j):
        return pltpu.make_async_copy(
            w_ref.at[i, :, pl.ds(j * kq, kq)], weights.at[:, pl.ds((2 * j + i) * kq, kq)], w_sem.at[i, j])

    def count_copy(r):
        return pltpu.make_async_remote_copy(
            src_ref=flags, dst_ref=counts.at[r - 1], send_sem=cnt_send.at[r - 1], recv_sem=cnt_recv.at[r - 1],
            device_id={"elem": lax.rem(me_e + r, ne)}, device_id_type=MESH)

    def chip(i):
        return lax.rem(mine + i, ways)

    def first_copy(u, i):
        rows = rows_of(u)
        return pltpu.make_async_remote_copy(
            src_ref=xpart.at[place(u), i - 1, 1 - core, rows], dst_ref=first.at[place(u), i - 1, rows],
            send_sem=first_send.at[u, i - 1], recv_sem=first_recv.at[u, i - 1],
            device_id={"elem": partner}, device_id_type=MESH)

    def second_copy(u, i):
        rows = rows_of(u)
        return pltpu.make_async_remote_copy(
            src_ref=first.at[place(u), i - 1, rows], dst_ref=second.at[place(u), i - 1, rows],
            send_sem=second_send.at[u, i - 1], recv_sem=second_recv.at[u, i - 1],
            device_id={"elem": 2 * chip(i) + core}, device_id_type=MESH)

    def own_copy(p):
        return pltpu.make_async_remote_copy(
            src_ref=opart.at[p, 1 - core], dst_ref=ofirst.at[p],
            send_sem=ofirst_send.at[p], recv_sem=ofirst_recv.at[p],
            device_id={"elem": partner}, device_id_type=MESH)

    own_in = pltpu.make_async_copy(s_ref, blocks.at[0], s_sem)
    flag_in = pltpu.make_async_copy(flag_ref, flags, f_sem)
    flag_in.start()
    own_in.start()

    barrier = pltpu.get_barrier_semaphore()
    for b in (ahead, behind):
        pl.semaphore_signal(barrier, inc=1, device_id={"beam": b}, device_id_type=MESH)
    for r in range(1, ne):
        pl.semaphore_signal(barrier, inc=1, device_id={"elem": lax.rem(me_e + r, ne)}, device_id_type=MESH)
    pl.semaphore_wait(barrier, 2 + ne - 1)

    arrived = {((0, 0), j) for j in range(q)}
    sent = [0, 0]

    def send_ready():
        for way in (0, 1):
            while sent[way] < len(arrivals[way]):
                d, j = arrivals[way][sent[way]]
                if d > 1 and ((way, d - 1), j) not in arrived:
                    break
                ring_copy(way, d, j).start()
                sent[way] += 1

    send_ready()
    for j in range(q):
        for i in (0, 1):
            weight_copy(i, j).start()

    flag_in.wait()
    for r in range(1, ne):
        count_copy(r).start()
    mask[...] = jnp.broadcast_to(flags[...].astype(jnp.float32).astype(jnp.bfloat16), mask.shape)
    own_in.wait()

    def right_of(block):
        return 0 if block == (0, half) else slot_of(*block) - (slot_of(*block) > half)

    def stage(block, j):
        slot, place = slot_of(*block), right_of(block)
        columns = pl.ds(j * kq, kq)
        re = blocks[slot, 0, :, columns] * mask[:, columns]
        im = blocks[slot, 1, :, columns] * mask[:, columns]
        left, right = pl.ds(2 * j * kq, kq), pl.ds((2 * j + 1) * kq, kq)
        rhs[place, :tb, left] = re
        rhs[place, tb:, left] = im
        rhs[place, :tb, right] = -im
        rhs[place, tb:, right] = re

    weights_here = set()

    def need(j0, j1):
        for j in range(j0, j1):
            if j not in weights_here:
                weights_here.add(j)
                for i in (0, 1):
                    weight_copy(i, j).wait()

    def apart(step):
        @pl.loop(0, 1 + me_e // ne)
        def _(_):
            step()

    def product(rows, columns, j0, j1):
        ks = pl.ds(2 * j0 * kq, 2 * (j1 - j0) * kq)
        right = jnp.concatenate([rhs[right_of(b), :, ks] for b in columns], axis=0)
        return lax.dot_general(weights[rows, ks], right, (((1,), (1,)), ((), ())),
                               preferred_element_type=jnp.float32)

    def put(ref, index, value, fresh):
        if fresh:
            ref[index] = value
        else:
            ref[index] += value

    def fold(value):
        lane = lax.broadcasted_iota(jnp.int32, (mo // 2, LANES), 1)
        return jnp.where(lane < blk, value[:mo // 2], value[mo // 2:])

    def x_store(u, i, o, value, fresh):
        put(xpart, (place(u), i - 1, o, rows_of(u)), fold(value) if folded(u) else value, fresh)

    def x_slice(d, j0, j1, fresh, final):
        need(j0, j1)
        units = units_of(d)
        columns = [b for u in units for b in unit_columns(u)]

        def part(i, o):
            rows = pl.ds(pl.multiple_of((2 * chip(i) + o) * mo, mo), mo)
            result = product(rows, columns, j0, j1)
            for n, u in enumerate(units):
                x_store(u, i, o, result[:, n * LANES:(n + 1) * LANES], fresh)

        def both(i):
            rows = pl.ds(pl.multiple_of(2 * chip(i) * mo, 2 * mo), 2 * mo)
            result = product(rows, columns, j0, j1)
            for n, u in enumerate(units):
                for o in (0, 1):
                    x_store(u, i, o, result[o * mo:(o + 1) * mo, n * LANES:(n + 1) * LANES], fresh)

        for i in range(1, ways):
            if final:
                apart(functools.partial(part, i, 1 - core))
                for u in units:
                    first_copy(u, i).start()
                apart(functools.partial(part, i, core))
            else:
                apart(functools.partial(both, i))

    def own_slice(g, j0, j1, fresh, final):
        need(j0, j1)
        pairs = [p for p in (2 * g, 2 * g + 1) if p < half]
        columns = [b for p in pairs for b in pair_columns(p)]

        def part(o):
            rows = pl.ds(pl.multiple_of((2 * mine + o) * mo, mo), mo)
            result = product(rows, columns, j0, j1)
            for n, p in enumerate(pairs):
                put(opart, (p, o), result[:, n * LANES:(n + 1) * LANES], fresh)

        def both():
            rows = pl.ds(pl.multiple_of(2 * mine * mo, 2 * mo), 2 * mo)
            result = product(rows, columns, j0, j1)
            for n, p in enumerate(pairs):
                for o in (0, 1):
                    put(opart, (p, o), result[o * mo:(o + 1) * mo, n * LANES:(n + 1) * LANES], fresh)

        if final:
            apart(functools.partial(part, 1 - core))
            for p in pairs:
                own_copy(p).start()
            apart(functools.partial(part, core))
        else:
            apart(both)

    def own_run(g, j0, j1):
        for j in range(j0, j1, step):
            own_slice(g, j, j + step, j == 0, j + step == q)

    def pass_on(d):
        for i in range(1, ways):
            for u in units_of(d):
                rows = rows_of(u)
                first_copy(u, i).wait_recv()
                first[place(u), i - 1, rows] += xpart[place(u), i - 1, core, rows]
                second_copy(u, i).start()

    def make_selection():
        row = lax.broadcasted_iota(jnp.int32, (blk, 2 * snaps), 0)
        column = lax.broadcasted_iota(jnp.int32, (blk, 2 * snaps), 1)
        offset = column - jnp.where(row < tb, row, row - tb + snaps)
        for p in range(half):
            for n, (way, d) in enumerate(pair_columns(p)):
                source = lookup(order, lax.rem(pos + (d if way else nb - d), nb))
                select[p * LANES + n * blk:p * LANES + (n + 1) * blk, :] = jnp.where(
                    offset == source * tb, 1.0, 0.0).astype(jnp.bfloat16)

    def live_gain():
        live = flags[...].astype(jnp.float32)
        for r in range(1, ne):
            count_copy(r).wait()
            live = live + counts[r - 1].astype(jnp.float32)
        return jnp.sqrt(jnp.float32(depth * ne) / jnp.sum(live, axis=1, keepdims=True))

    received = set()

    def unit_sum(u):
        for i in range(1, ways):
            if (u, i) not in received:
                received.add((u, i))
                second_copy(u, i).wait_recv()
        total = second[place(u), 0, rows_of(u)]
        for i in range(2, ways):
            total = total + second[place(u), i - 1, rows_of(u)]
        return total

    def finish(p, gain):
        own_copy(p).wait_recv()
        total = opart[p, core] + ofirst[p]
        if p == 0:
            total = total + unit_sum(0)
        else:
            left, right = unit_sum(p), unit_sum(p + 1)
            if folded(p):
                left = jnp.concatenate([left, pltpu.roll(left, blk, 1)], axis=0)
            if folded(p + 1):
                right = jnp.concatenate([pltpu.roll(right, blk, 1), right], axis=0)
            lane = lax.broadcasted_iota(jnp.int32, (mo, LANES), 1)
            total = total + jnp.where(lane < blk, left, right)
        total = total * gain
        put(square, (slice(None), slice(None)), total * total, p == 0)
        values[:, p * LANES:(p + 1) * LANES] = total.astype(jnp.bfloat16)

    gain = None
    groups = (half + 1) // 2
    make_selection()
    for k in range(len(arrivals[0])):
        for way in (0, 1):
            d, j = arrivals[way][k]
            ring_copy(way, d, j).wait_recv()
            arrived.add(((0 if d == half else way, d), j))
            send_ready()
        d, j = arrivals[1][k]
        if j == 0 and d > 1:
            pass_on(d - 1)
        if d < half:
            if d == 1:
                stage((0, 0), j)
            stage((0, d), j)
            stage((1, d), j)
            if (j + 1) % step == 0:
                x_slice(d, j + 1 - step, j + 1, j + 1 == step, j == q - 1)
            if d % 2 == 0 and j == q - 1 and d // 2 < groups:
                own_run(d // 2 - 1, 0, q // 2)
            if d % 2 == 1 and d > 1 and j == q // 2 - 1:
                own_run((d - 3) // 2, q // 2, q)
            if j == q - 1 and d >= 3:
                if gain is None:
                    gain = live_gain()
                for p in range(half - 2):
                    if min(p + 3, half - 1) == d:
                        finish(p, gain)
        else:
            m = j
            stage((0, half), m)
            stage((0, half), q - 1 - m)
            if m < q // 2 - 1:
                x_slice(half, m, m + 1, m == 0, False)
                x_slice(half, q - 1 - m, q - m, False, False)
            else:
                x_slice(half, m, m + 2, m == 0, True)

    pass_on(half)
    own_run(groups - 1, 0, q)
    if gain is None:
        gain = live_gain()
    for p in range(max(0, half - 2), half):
        finish(p, gain)
    for part in (0, 1):
        for rows in (slice(0, mo // 2), slice(mo // 2, mo)):
            out_ref[part, rows] = jnp.dot(values[rows], select[:, part * snaps:(part + 1) * snaps],
                                          preferred_element_type=jnp.float32).astype(jnp.bfloat16)
    power = jnp.sum(square[...].T, axis=0, keepdims=True) * (1.0 / snaps)
    pow_ref[...] = power

    for way in (0, 1):
        for d, j in arrivals[way]:
            ring_copy(way, d, j).wait_send()
    for u in range(half + 1):
        for i in range(1, ways):
            first_copy(u, i).wait_send()
            second_copy(u, i).wait_send()
    for p in range(half):
        own_copy(p).wait_send()


def body(order, ne, signals, weights, element_flags):
    nb = len(order)
    half = nb // 2
    _, depth, tb = signals.shape
    rows = weights.shape[1]
    mo = rows // ne
    q = PIECES
    ways = ne // 2
    if nb % 4 or ne % 2 or ways < 2 or 4 * tb != LANES:
        raise ValueError("unsupported mesh")
    items = q * (half - 1) + q // 2
    dma = pltpu.SemaphoreType.DMA
    anywhere = pl.BlockSpec(memory_space=pltpu.MemorySpace.HBM)
    vmem = pl.BlockSpec(memory_space=pltpu.VMEM)
    out, power = pl.pallas_call(
        functools.partial(kernel, order, ne),
        out_shape=(jax.ShapeDtypeStruct((2, mo, nb * tb), jnp.bfloat16),
                   jax.ShapeDtypeStruct((1, mo), jnp.float32)),
        in_specs=[anywhere, anywhere, anywhere],
        out_specs=(vmem, vmem),
        scratch_shapes=[
            pltpu.VMEM((nb, 2, tb, depth), jnp.bfloat16),
            pltpu.VMEM((1, depth), jnp.int32),
            pltpu.VMEM((tb, depth), jnp.bfloat16),
            pltpu.VMEM((rows, 2 * depth), jnp.bfloat16),
            pltpu.VMEM((nb - 1, 2 * tb, 2 * depth), jnp.bfloat16),
            pltpu.VMEM((half, ways - 1, 2, mo, LANES), jnp.float32),
            pltpu.VMEM((half, 2, mo, LANES), jnp.float32),
            pltpu.VMEM((half, ways - 1, mo, LANES), jnp.float32),
            pltpu.VMEM((half, mo, LANES), jnp.float32),
            pltpu.VMEM((half, ways - 1, mo, LANES), jnp.float32),
            pltpu.VMEM((ne - 1, 1, depth), jnp.int32),
            pltpu.VMEM((half * LANES, 2 * nb * tb), jnp.bfloat16),
            pltpu.VMEM((mo, half * LANES), jnp.bfloat16),
            pltpu.VMEM((mo, LANES), jnp.float32),
            dma((2, items)), dma((2, items)), dma((2, q)), dma, dma,
            dma((half + 1, ways - 1)), dma((half + 1, ways - 1)), dma((half,)), dma((half,)),
            dma((half + 1, ways - 1)), dma((half + 1, ways - 1)),
            dma((ne - 1,)), dma((ne - 1,)),
        ],
        compiler_params=pltpu.CompilerParams(
            collective_id=0, has_side_effects=True, vmem_limit_bytes=53 * 2**20),
        name="beamform",
    )(signals.transpose(0, 2, 1), element_flags.reshape(1, depth), weights)
    return out, power.reshape(mo)


def solution(mesh):
    return jax.shard_map(
        functools.partial(body, ring_order(mesh), mesh.shape["elem"]),
        mesh=mesh,
        in_specs=(P(None, "elem", "beam"), P(None, "beam", "elem"), P("elem")),
        out_specs=(P(None, ("beam", "elem"), None), P(("beam", "elem"))),
        check_vma=False,
    )
```

time: 67.9 us -> 62 us (0.913)
  Pallas kernels: 63.9 us -> 59 us
  local copies, waits for them, and re-layouts: 3.13 us -> 2.08 us
    pallas_call x1, Pallas kernels: 63.9 us -> 59 us  [body(): pl.pallas_call(functools.partial(kernel, order, ne), out_shape=(jax.Shape...]
    unnamed x6 -> x4, local copies, waits for them, and re-layouts: 3.13 us -> 2.08 us
where the time goes in v1:
time: 62 us; the launch traced here: 61.8 us
  Pallas kernels  59 us (95%)
  local copies, waits for them, and re-layouts  2.08 us (3%)
  between operations  0.65 us (1%)
    pallas_call x1, Pallas kernels, body(): pl.pallas_call(functools.partial(kernel, order, ne), out_shape=(jax.Shape...  59 us
    unnamed x4, local copies, waits for them, and re-layouts  2.08 us

profile of v1, /device:TPU:0, one launch (start us, length us, event | category | flops | bytes accessed | tf_op | source)
XLA Modules:
  0.0 61.8 jit_solution(9592525172905619783)
XLA Ops:
  0.6 0.0 copy-start
  0.6 0.7 %copy-done = s32[4096]{0:T(1024)S(1)} copy-done((s32[4096]{0:T(1024)S(1)}, s32[4096]{0:T(1024)}, u32[]{:S(2)}) %copy-start) | copy-done | bytes 16408
  1.3 59.0 %beamform.1 = (bf16[2,512,256]{2,1,0:T(8,128)(2,1)S(1)}, f32[1,512]{1,0:T(1,128)S(1)}) custom-call(bf16[2,32,4096]{2,1,0:T(8,128)(2,1)} %bitcast.5, s32[1,4096]{1,0:T(1,128)S(1)} %bitcast.3, bf16[2,2048,4096]{2,1,0:T(8,128)(2,1)} %w_ref.1), custom_call_target="tpu_custom_call" | custom-call | tf_op jit(solution)/shard_map/beamform/pallas_call | solution.py:413
  60.4 0.8 %copy.7 = bf16[2,512,256]{2,1,0:T(8,128)(2,1)} copy(bf16[2,512,256]{2,1,0:T(8,128)(2,1)S(1)} %get-tuple-element.8) | data formatting | bytes 1048576
  61.2 0.6 copy.8
Async XLA Ops:
  0.6 0.7 %copy-start = (s32[4096]{0:T(1024)S(1)}, s32[4096]{0:T(1024)}, u32[]{:S(2)}) copy-start(s32[4096]{0:T(1024)} %param.5) | copy-start | bytes 49156

commit v2 on v1

--- a/solution.py
+++ b/solution.py
@@ -97,13 +97,13 @@
 
     low, high = q // 2, q // 2
     arrivals = [[(d, j) for d in range(1, half) for j in range(q)] + [(half, j) for j in last]
-                for last in (range(q - 1, high - 1, -1), range(low))]
+                for last in ([*range(high + 1, q), high], range(low))]
     number = [{item: k for k, item in enumerate(a)} for a in arrivals]
 
     def ring_copy(way, d, j):
         k = number[way][(d, j)]
         return pltpu.make_async_remote_copy(
-            src_ref=(s_ref if d == 1 else blocks.at[slot_of(way, d - 1)]).at[:, :, pl.ds(j * kq, kq)],
+            src_ref=blocks.at[0 if d == 1 else slot_of(way, d - 1)].at[:, :, pl.ds(j * kq, kq)],
             dst_ref=blocks.at[slot_of(way, d), :, :, pl.ds(j * kq, kq)],
             send_sem=ring_send.at[way, k], recv_sem=ring_recv.at[way, k],
             device_id={"beam": ahead if way == 0 else behind}, device_id_type=MESH)
@@ -142,14 +142,18 @@
 
     own_in = pltpu.make_async_copy(s_ref, blocks.at[0], s_sem)
     flag_in = pltpu.make_async_copy(flag_ref, flags, f_sem)
+    own_in.start()
     flag_in.start()
-    own_in.start()
+    for j in range(q):
+        for i in (0, 1):
+            weight_copy(i, j).start()
 
     barrier = pltpu.get_barrier_semaphore()
     for b in (ahead, behind):
         pl.semaphore_signal(barrier, inc=1, device_id={"beam": b}, device_id_type=MESH)
     for r in range(1, ne):
         pl.semaphore_signal(barrier, inc=1, device_id={"elem": lax.rem(me_e + r, ne)}, device_id_type=MESH)
+    own_in.wait()
     pl.semaphore_wait(barrier, 2 + ne - 1)
 
     arrived = {((0, 0), j) for j in range(q)}
@@ -165,15 +169,10 @@
                 sent[way] += 1
 
     send_ready()
-    for j in range(q):
-        for i in (0, 1):
-            weight_copy(i, j).start()
-
     flag_in.wait()
     for r in range(1, ne):
         count_copy(r).start()
     mask[...] = jnp.broadcast_to(flags[...].astype(jnp.float32).astype(jnp.bfloat16), mask.shape)
-    own_in.wait()
 
     def right_of(block):
         return 0 if block == (0, half) else slot_of(*block) - (slot_of(*block) > half)
@@ -249,14 +248,15 @@
             else:
                 apart(functools.partial(both, i))
 
-    def own_slice(g, j0, j1, fresh, final):
+    def own_slice(g, j0, j1, fresh, final, cuts=1):
         need(j0, j1)
+        size = (j1 - j0) // cuts
         pairs = [p for p in (2 * g, 2 * g + 1) if p < half]
         columns = [b for p in pairs for b in pair_columns(p)]
 
-        def part(o):
+        def part(o, j):
             rows = pl.ds(pl.multiple_of((2 * mine + o) * mo, mo), mo)
-            result = product(rows, columns, j0, j1)
+            result = product(rows, columns, j, j + size)
             for n, p in enumerate(pairs):
                 put(opart, (p, o), result[:, n * LANES:(n + 1) * LANES], fresh)
 
@@ -268,10 +268,12 @@
                     put(opart, (p, o), result[o * mo:(o + 1) * mo, n * LANES:(n + 1) * LANES], fresh)
 
         if final:
-            apart(functools.partial(part, 1 - core))
+            for j in range(j0, j1, size):
+                apart(functools.partial(part, 1 - core, j))
             for p in pairs:
                 own_copy(p).start()
-            apart(functools.partial(part, core))
+            for j in range(j0, j1, size):
+                apart(functools.partial(part, core, j))
         else:
             apart(both)
 
@@ -333,6 +335,12 @@
         put(square, (slice(None), slice(None)), total * total, p == 0)
         values[:, p * LANES:(p + 1) * LANES] = total.astype(jnp.bfloat16)
 
+    def sends_done(d):
+        for way in (0, 1):
+            for item in arrivals[way]:
+                if item[0] == d:
+                    ring_copy(way, *item).wait_send()
+
     gain = None
     groups = (half + 1) // 2
     make_selection()
@@ -343,8 +351,6 @@
             arrived.add(((0 if d == half else way, d), j))
             send_ready()
         d, j = arrivals[1][k]
-        if j == 0 and d > 1:
-            pass_on(d - 1)
         if d < half:
             if d == 1:
                 stage((0, 0), j)
@@ -362,18 +368,27 @@
                 for p in range(half - 2):
                     if min(p + 3, half - 1) == d:
                         finish(p, gain)
+            if j == q - 1:
+                pass_on(d)
+                sends_done(d - 1)
         else:
-            m = j
+            m, n = j, arrivals[0][k][1]
             stage((0, half), m)
-            stage((0, half), q - 1 - m)
-            if m < q // 2 - 1:
+            stage((0, half), n)
+            if n > high:
                 x_slice(half, m, m + 1, m == 0, False)
-                x_slice(half, q - 1 - m, q - m, False, False)
+                x_slice(half, n, n + 1, False, False)
             else:
                 x_slice(half, m, m + 2, m == 0, True)
 
     pass_on(half)
-    own_run(groups - 1, 0, q)
+    own_run(groups - 1, 0, q // 2)
+    own_slice(groups - 1, q // 2, q, False, True, 2)
+    for d in (half - 1, half):
+        sends_done(d)
+    for u in range(half + 1):
+        for i in range(1, ways):
+            first_copy(u, i).wait_send()
     if gain is None:
         gain = live_gain()
     for p in range(max(0, half - 2), half):
@@ -385,12 +400,8 @@
     power = jnp.sum(square[...].T, axis=0, keepdims=True) * (1.0 / snaps)
     pow_ref[...] = power
 
-    for way in (0, 1):
-        for d, j in arrivals[way]:
-            ring_copy(way, d, j).wait_send()
     for u in range(half + 1):
         for i in range(1, ways):
-            first_copy(u, i).wait_send()
             second_copy(u, i).wait_send()
     for p in range(half):
         own_copy(p).wait_send()

time: 62 us -> 59.9 us (0.966)
  Pallas kernels: 59 us -> 56.9 us
    pallas_call x1, Pallas kernels: 59 us -> 56.9 us  [body(): pl.pallas_call(functools.partial(kernel, order, ne), out_shape=(jax.Shape...]
where the time goes in v2:
time: 59.9 us; the launch traced here: 59.6 us
  Pallas kernels  56.9 us (95%)
  local copies, waits for them, and re-layouts  2.08 us (3%)
  between operations  0.65 us (1%)
    pallas_call x1, Pallas kernels, body(): pl.pallas_call(functools.partial(kernel, order, ne), out_shape=(jax.Shape...  56.9 us
    unnamed x4, local copies, waits for them, and re-layouts  2.08 us

profile of v2, /device:TPU:0, one launch (start us, length us, event | category | flops | bytes accessed | tf_op | source)
XLA Modules:
  0.0 59.6 jit_solution(2011101191712222809)
XLA Ops:
  0.6 0.0 copy-start
  0.6 0.7 %copy-done = s32[4096]{0:T(1024)S(1)} copy-done((s32[4096]{0:T(1024)S(1)}, s32[4096]{0:T(1024)}, u32[]{:S(2)}) %copy-start) | copy-done | bytes 16408
  1.3 56.9 %beamform.1 = (bf16[2,512,256]{2,1,0:T(8,128)(2,1)S(1)}, f32[1,512]{1,0:T(1,128)S(1)}) custom-call(bf16[2,32,4096]{2,1,0:T(8,128)(2,1)} %bitcast.5, s32[1,4096]{1,0:T(1,128)S(1)} %bitcast.3, bf16[2,2048,4096]{2,1,0:T(8,128)(2,1)} %w_ref.1), custom_call_target="tpu_custom_call" | custom-call | tf_op jit(solution)/shard_map/beamform/pallas_call | solution.py:424
  58.2 0.8 %copy.7 = bf16[2,512,256]{2,1,0:T(8,128)(2,1)} copy(bf16[2,512,256]{2,1,0:T(8,128)(2,1)S(1)} %get-tuple-element.8) | data formatting | bytes 1048576
  59.0 0.6 copy.8
Async XLA Ops:
  0.6 0.7 %copy-start = (s32[4096]{0:T(1024)S(1)}, s32[4096]{0:T(1024)}, u32[]{:S(2)}) copy-start(s32[4096]{0:T(1024)} %param.5) | copy-start | bytes 49156

commit v3 on v2

--- a/solution.py
+++ b/solution.py
@@ -142,18 +142,19 @@
 
     own_in = pltpu.make_async_copy(s_ref, blocks.at[0], s_sem)
     flag_in = pltpu.make_async_copy(flag_ref, flags, f_sem)
+    flag_in.start()
     own_in.start()
-    flag_in.start()
-    for j in range(q):
-        for i in (0, 1):
-            weight_copy(i, j).start()
 
     barrier = pltpu.get_barrier_semaphore()
     for b in (ahead, behind):
         pl.semaphore_signal(barrier, inc=1, device_id={"beam": b}, device_id_type=MESH)
     for r in range(1, ne):
         pl.semaphore_signal(barrier, inc=1, device_id={"elem": lax.rem(me_e + r, ne)}, device_id_type=MESH)
+    flag_in.wait()
     own_in.wait()
+    for j in range(q):
+        for i in (0, 1):
+            weight_copy(i, j).start()
     pl.semaphore_wait(barrier, 2 + ne - 1)
 
     arrived = {((0, 0), j) for j in range(q)}
@@ -169,7 +170,6 @@
                 sent[way] += 1
 
     send_ready()
-    flag_in.wait()
     for r in range(1, ne):
         count_copy(r).start()
     mask[...] = jnp.broadcast_to(flags[...].astype(jnp.float32).astype(jnp.bfloat16), mask.shape)
@@ -450,7 +450,8 @@
         compiler_params=pltpu.CompilerParams(
             collective_id=0, has_side_effects=True, vmem_limit_bytes=53 * 2**20),
         name="beamform",
-    )(signals.transpose(0, 2, 1), element_flags.reshape(1, depth), weights)
+    )(signals.transpose(0, 2, 1),
+      pltpu.with_memory_space_constraint(element_flags.reshape(1, depth), pltpu.MemorySpace.HBM), weights)
     return out, power.reshape(mo)
 
 

time: 59.9 us -> 59.1 us (0.987)
  local copies, waits for them, and re-layouts: 2.08 us -> 1.37 us
    unnamed x4 -> x2, local copies, waits for them, and re-layouts: 2.08 us -> 1.37 us
where the time goes in v3:
time: 59.1 us; the launch traced here: 58.9 us
  Pallas kernels  56.9 us (96%)
  local copies, waits for them, and re-layouts  1.37 us (2%)
  between operations  0.64 us (1%)
    pallas_call x1, Pallas kernels, body(): pl.pallas_call(functools.partial(kernel, order, ne), out_shape=(jax.Shape...  56.9 us
    unnamed x2, local copies, waits for them, and re-layouts  1.37 us

profile of v3, /device:TPU:0, one launch (start us, length us, event | category | flops | bytes accessed | tf_op | source)
XLA Modules:
  0.0 58.9 jit_solution(1688499156181942981)
XLA Ops:
  0.6 56.9 %beamform.1 = (bf16[2,512,256]{2,1,0:T(8,128)(2,1)S(1)}, f32[1,512]{1,0:T(1,128)S(1)}) custom-call(bf16[2,32,4096]{2,1,0:T(8,128)(2,1)} %bitcast.4, s32[1,4096]{1,0:T(1,128)} %bitcast.5, bf16[2,2048,4096]{2,1,0:T(8,128)(2,1)} %w_ref.1), custom_call_target="tpu_custom_call" | custom-call | tf_op jit(solution)/shard_map/beamform/pallas_call | solution.py:424
  57.5 0.8 %copy.7 = bf16[2,512,256]{2,1,0:T(8,128)(2,1)} copy(bf16[2,512,256]{2,1,0:T(8,128)(2,1)S(1)} %get-tuple-element.8) | data formatting | bytes 1048576
  58.3 0.6 copy.8
